TPU v7x, 32 devices: a whole 2x2x4 slice. The times are simulated.
32 devices in a mesh: stn: 8 (over z, x), chan: 4 (over y, core).
Axes of the slice: x: 2, y: 2, z: 4, core: 2. Of those that a mesh axis runs over, the one named last changes fastest.
Arguments:
- samples: bfloat16 [64, 17, 2, 8192], P(('stn', 'chan')), may hold values from -6 to 6
- keeper: int32 [8, 8], replicated, may hold values from 0 to 1, as said below
Outputs:
- visibilities: bfloat16 [64, 2, 4096, 40], P('stn', None, 'chan')
Inputs may be any that keep to these rules, and one draw needn't show every extreme that they name: keeper[g, g] is 1; for g != h with d = (g - h) mod 8: keeper[g, h] is 1 where 0 < d < 4, 0 where d > 4, and at d = 4 exactly one of keeper[g, h] and keeper[h, g] is 1, which one drawn for each such pair; half of the rows hold 5 ones, the others 5 - 1.
All inputs are finite; a program needn't handle non-finite values.
Results may differ from a plain program's by a relative error of at most 0.0077.
Values may be sent and summed in bfloat16 or wider, within the bound.
A program may use at most 192 MiB of HBM per device.

v0:
```python
import math
import jax
import jax.numpy as jnp
from jax import lax
from jax.sharding import PartitionSpec as P

NFFT = 8192
TAPS = 16
CH_WIN = 1024
DFT_BLOCK = 256


def from_behind(value, axis, by):
    devices = lax.axis_size(axis)
    return lax.ppermute(value, axis, [(i, (i + by) % devices) for i in range(devices)])


def taps_table():
    pos = jnp.arange(TAPS * NFFT).astype(jnp.float32)
    shifted = (pos + 0.5) / NFFT - TAPS / 2.0
    window = 0.5 - 0.5 * jnp.cos(2.0 * math.pi * (pos + 0.5) / (TAPS * NFFT))
    return (jnp.sinc(shifted) * window).reshape(TAPS, NFFT)


def twiddles(width):
    index_n = jnp.arange(NFFT, dtype=jnp.int32)[:, None]
    index_k = jnp.arange(width, dtype=jnp.int32)[None, :]
    phase = (index_n * index_k % NFFT).astype(jnp.float32) * (2.0 * math.pi / NFFT)
    cosines = jnp.cos(phase).astype(jnp.bfloat16)
    sines = jnp.sin(phase).astype(jnp.bfloat16)
    upper = jnp.concatenate([cosines, -sines], axis=1)
    lower = jnp.concatenate([sines, cosines], axis=1)
    return jnp.concatenate([upper, lower], axis=0)


def rotations(ch_tot, width):
    blocks = ch_tot // width
    index_n = jnp.arange(NFFT, dtype=jnp.int32)[None, :]
    index_b = jnp.arange(blocks, dtype=jnp.int32)[:, None]
    phase = (index_n * index_b * width % NFFT).astype(jnp.float32) * (2.0 * math.pi / NFFT)
    return (jnp.cos(phase), jnp.sin(phase))


def channelise(block, taps, table, cos_rot, sin_rot, ch_tot):
    frames = block.shape[1] - TAPS + 1
    count = block.shape[0]
    width = table.shape[1] // 2
    blocks = ch_tot // width
    total = taps[0] * block[:, 0:frames].astype(jnp.float32)
    for tap in range(1, TAPS):
        total = total + taps[tap] * block[:, tap : tap + frames].astype(jnp.float32)
    real_part = total[:, :, 0][None]
    imag_part = total[:, :, 1][None]
    cosine = cos_rot[:, None, None, :]
    sine = sin_rot[:, None, None, :]
    rot_real = real_part * cosine + imag_part * sine
    rot_imag = imag_part * cosine - real_part * sine
    lhs = jnp.stack([rot_real, rot_imag], axis=3).astype(jnp.bfloat16)
    lhs = lhs.reshape(blocks * count * frames, 2 * NFFT)
    spectrum = jnp.dot(lhs, table, preferred_element_type=jnp.float32) * (1.0 / math.sqrt(NFFT))
    spectrum = spectrum.astype(jnp.bfloat16).reshape(blocks, count, frames, 2, width)
    spectrum = jnp.transpose(spectrum, (1, 0, 4, 3, 2))
    return spectrum.reshape(count, ch_tot, 2, frames)


def correlate(own, others, frames):
    half = others.shape[2] // 2
    turned = jnp.concatenate([-others[:, :, half:], others[:, :, :half]], axis=2)
    rhs = jnp.concatenate([others, turned], axis=0)
    product = lax.dot_general(
        own, rhs, (((2,), (2,)), ((1,), (1,))), preferred_element_type=jnp.float32
    )
    rows = others.shape[0]
    product = product.reshape(product.shape[0], product.shape[1], 2, rows)
    return jnp.transpose(product, (1, 2, 0, 3)) / frames


def slot_table(keep_rows, keep_slots):
    ranking = jnp.cumsum(keep_rows, axis=1) - 1
    slot_index = jnp.arange(keep_slots, dtype=jnp.int32)
    matched = (keep_rows[:, :, None] == 1) & (ranking[:, :, None] == slot_index[None, None, :])
    column_ids = jnp.arange(keep_rows.shape[1], dtype=jnp.int32)
    slot_column = jnp.sum(jnp.where(matched, column_ids[None, :, None], 0), axis=1)
    filled = jnp.any(matched, axis=1)
    return (slot_column, filled)


def per_device(samples, keeper):
    n_chan = lax.axis_size("chan")
    n_stn = lax.axis_size("stn")
    ch_tot = CH_WIN * n_chan
    frames = samples.shape[1] - TAPS + 1
    cos_rot, sin_rot = rotations(ch_tot, DFT_BLOCK)
    spectrum = channelise(samples, taps_table(), twiddles(DFT_BLOCK), cos_rot, sin_rot, ch_tot)
    local = lax.all_to_all(spectrum, "chan", split_axis=1, concat_axis=0, tiled=True)
    group_in = local.shape[0]
    own = local.reshape(group_in, CH_WIN, 2 * frames)
    keep_slots = n_stn // 2 + 1
    group_index = lax.axis_index("stn")
    row_keep = jnp.take(keeper, group_index, axis=0)
    slot_column, filled = slot_table(row_keep[None], keep_slots)
    slot_column = slot_column[0]
    filled = filled[0]
    nothing = jnp.zeros((), jnp.bfloat16)
    half = n_stn // 2
    stacked = own[None]
    stride = 1
    while stride < half:
        moved = from_behind(stacked, "stn", stride)
        stacked = jnp.concatenate([stacked, moved], axis=0)
        stride = stride * 2
    far_group = from_behind(own, "stn", half)
    partners = jnp.concatenate([stacked, far_group[None]], axis=0)
    partners = partners.reshape((half + 1) * group_in, CH_WIN, 2 * frames)
    tiles = correlate(own, partners, frames).astype(jnp.bfloat16)
    tiles = tiles.reshape(group_in, 2, CH_WIN, half + 1, group_in)
    slot_distance = jnp.minimum((group_index - slot_column) % n_stn, half)
    picked = jnp.take(tiles, slot_distance, axis=3)
    picked = jnp.where(filled[None, None, None, :, None], picked, nothing)
    return picked.reshape(group_in, 2, CH_WIN, keep_slots * group_in)


def solution(mesh):
    placed = (P(("stn", "chan"), None, None, None), P())
    return jax.shard_map(
        per_device,
        mesh=mesh,
        in_specs=placed,
        out_specs=P("stn", None, "chan", None),
        check_vma=False,
    )
```

profile of v0, /device:TPU:0, one launch (start us, length us, event | category | flops | bytes accessed | tf_op | source)
XLA Modules:
  0.0 166.4 jit_solution(14174221383164325046)
XLA Ops:
  0.0 2.4 %fusion.29 = f32[131072]{0:T(1024)S(1)} fusion(), kind=kLoop, calls=%fused_computation.45 | loop fusion | flops 5373952 | bytes 524288 | tf_op jit(solution)/shard_map/mul | solution.py:22
  2.4 2.1 %fusion.41 = (f32[16,8192]{1,0:T(8,128)S(1)}, f32[16,8192]{1,0:T(8,128)S(1)}) fusion(), kind=kLoop, calls=%fused_computation.65 | loop fusion | flops 1966080 | bytes 1048576 | tf_op jit(solution)/shard_map/sin | solution.py:41
  4.5 35.0 %sine_convert_fusion = (bf16[8192,256]{1,0:T(8,128)(2,1)}, bf16[8192,256]{1,0:T(8,128)(2,1)}) fusion(), kind=kLoop, calls=%fused_computation.15 | loop fusion | flops 33554432 | bytes 8388608 | tf_op jit(solution)/shard_map/convert_element_type | solution.py:30
  39.5 32.3 %fusion.14 = bf16[8192,256]{1,0:T(8,128)(2,1)} fusion(), kind=kLoop, calls=%fused_computation.24 | loop fusion | flops 37748736 | bytes 4194304 | tf_op jit(solution)/shard_map/neg | solution.py:31
  71.9 2.1 %multiply_add_fusion.1 = f32[2,2,2,8192]{3,2,1,0:T(2,128)S(1)} fusion(bf16[2,17,2,8192]{3,2,1,0:T(2,128)(2,1)S(1)} %copy-done, f32[8192]{0:T(1024)S(1)} %get-tuple-element.19, f32[8192]{0:T(1024)S(1)} %get-tuple-element.20, f32[8192]{0:T(1024)S(1)} %get-tuple-element.21, f32[8192]{0:T(1024)S(1)} %get-tuple-element.22, f32[8192]{0:T(1024)S(1)} %get-tuple-element.23, ...), kind=kLoop, calls=%fused_computation.67 | loop fusion | flops 3080192 | bytes 2883584 | tf_op jit(solution)/shard_map/add | solution.py:51
  74.0 0.2 fusion.53
  74.2 0.2 copy_bitcast_fusion.1
  74.4 4.4 %add_convert_fusion = (bf16[16,2,2,1,8192]{4,3,2,1,0:T(2,128)(2,1)S(1)}, bf16[16,2,2,1,8192]{4,3,2,1,0:T(2,128)(2,1)S(1)}) fusion(f32[16,8192]{1,0:T(8,128)S(1)} %get-tuple-element.40, f32[2,2,8192]{2,1,0:T(2,128)S(1)} %get-tuple-element.38, f32[16,8192]{1,0:T(8,128)S(1)} %get-tuple-element.41, f32[2,2,8192]{2,1,0:T(2,128)S(1)} %get-tuple-element.39), kind=kLoop, calls=%fused_computation.23 | loop fusion | flops 4194304 | bytes 3407872 | tf_op jit(solution)/shard_map/convert
  78.8 4.8 %pad_maximum_fusion = bf16[16,2,2,2,8192]{4,3,2,1,0:T(2,128)(2,1)S(1)} fusion(bf16[16,2,2,1,8192]{4,3,2,1,0:T(2,128)(2,1)S(1)} %get-tuple-element.17, bf16[16,2,2,1,8192]{4,3,2,1,0:T(2,128)(2,1)S(1)} %get-tuple-element.16), kind=kLoop, calls=%fused_computation.21 | loop fusion | flops 4194304 | bytes 4194304 | tf_op jit(solution)/shard_map/stack | solution.py:58
  83.7 1.2 copy.55
  84.8 13.7 %fusion.19 = bf16[64,512]{1,0:T(8,128)(2,1)S(1)} fusion(bf16[64,16384]{1,0:T(8,128)(2,1)S(1)} %bitcast.50, bf16[8192,256]{1,0:T(8,128)(2,1)} %get-tuple-element.43, bf16[8192,256]{1,0:T(8,128)(2,1)} %get-tuple-element.42, bf16[8192,256]{1,0:T(8,128)(2,1)} %fusion.14), kind=kOutput, calls=%fused_computation.28 | convolution fusion | flops 1140916224 | bytes 14745600 | tf_op jit(solution)/shard_map/dot_general | solution.py:60
  98.6 4.9 %copy.50 = bf16[2,16,256,2,2]{4,3,0,2,1:T(2,128)(2,1)} copy(bf16[2,16,256,2,2]{2,1,4,3,0:T(8,128)(2,1)S(1)} %bitcast.51) | data formatting | bytes 131072 | tf_op jit(solution)/shard_map/reshape | solution.py:63
  103.6 7.8 %reshape.394 = bf16[4,2,4096]{2,1,0:T(2,128)(2,1)} reshape(bf16[4096,2,2,2]{3,2,1,0:T(2,128)(2,1)} %bitcast.46) | data formatting | bytes 131072
  111.3 4.3 %all-to-all-start = ((bf16[4,2,4096]{2,1,0:T(2,128)(2,1)}), bf16[4,2,4096]{2,1,0:T(2,128)(2,1)S(1)}, u32[]{:S(2)}, u32[]{:S(2)}) async-start(bf16[4,2,4096]{2,1,0:T(2,128)(2,1)} %reshape.394), calls=%async_computation | async-start | bytes 131072 | tf_op jit(solution)/shard_map/all_to_all | solution.py:95
  115.6 0.7 fusion.51
  116.3 0.7 compare_bitcast_fusion
  117.2 0.2 select_reduce_fusion
  117.4 2.3 %all-to-all-done = bf16[4,2,4096]{2,1,0:T(2,128)(2,1)S(1)} async-done(((bf16[4,2,4096]{2,1,0:T(2,128)(2,1)}), bf16[4,2,4096]{2,1,0:T(2,128)(2,1)S(1)}, u32[]{:S(2)}, u32[]{:S(2)}) %all-to-all-start) | async-done | bytes 65568 | tf_op jit(solution)/shard_map/all_to_all | solution.py:95
  119.7 10.0 %reshape.395 = bf16[4096,2,2,2]{3,2,1,0:T(2,128)(2,1)} reshape(bf16[4,2,4096]{2,1,0:T(2,128)(2,1)S(1)} %all-to-all-done) | data formatting | bytes 131072
  129.7 9.7 %copy.51 = bf16[2,4,1024,2,2]{2,1,4,3,0:T(4,128)(2,1)S(1)} copy(bf16[2,4,1024,2,2]{4,3,0,2,1:T(2,128)(2,1)} %bitcast.47) | data formatting | bytes 131072 | tf_op jit(solution)/shard_map/all_to_all | solution.py:95
  139.6 2.0 %collective-permute-start = (bf16[1,8,1024,4]{2,1,3,0:T(8,128)(2,1)S(1)}, bf16[1,8,1024,4]{2,1,3,0:T(8,128)(2,1)S(1)}, u32[]{:S(2)}, u32[]{:S(2)}) collective-permute-start(bf16[1,8,1024,4]{2,1,3,0:T(8,128)(2,1)S(1)} %broadcast_in_dim_reshape.3), channel_id=1, source_target_pairs={{0,4},{4,8},{8,12},{12,16},{16,20},{20,24},{24,28},{28,0},{1,5},{5... | collective-permute-start | bytes 196616 | tf_op jit(solution)/shard_map/ppermute | solution.py:15
  141.6 5.3 %collective-permute-done = bf16[1,8,1024,4]{2,1,3,0:T(8,128)(2,1)S(1)} collective-permute-done((bf16[1,8,1024,4]{2,1,3,0:T(8,128)(2,1)S(1)}, bf16[1,8,1024,4]{2,1,3,0:T(8,128)(2,1)S(1)}, u32[]{:S(2)}, u32[]{:S(2)}) %collective-permute-start) | collective-permute-done | bytes 65568 | tf_op jit(solution)/shard_map/ppermute | solution.py:15
  147.0 0.2 fusion.43
  147.5 2.6 %collective-permute-start.2 = (bf16[8,1024,4]{1,0,2:T(8,128)(2,1)S(1)}, bf16[8,1024,4]{1,0,2:T(8,128)(2,1)S(1)}, u32[]{:S(2)}, u32[]{:S(2)}) collective-permute-start(bf16[8,1024,4]{1,0,2:T(8,128)(2,1)S(1)} %reshape.350), channel_id=1, source_target_pairs={{0,16},{4,20},{8,24},{12,28},{16,0},{20,4},{24,8},{28,12},{1,17},{... | collective-permute-start | bytes 196616 | tf_op jit(solution)/shard_map/ppermute | solution.py:15
  150.1 1.4 copy.46
  151.5 4.0 %collective-permute-done.2 = bf16[8,1024,4]{1,0,2:T(8,128)(2,1)S(1)} collective-permute-done((bf16[8,1024,4]{1,0,2:T(8,128)(2,1)S(1)}, bf16[8,1024,4]{1,0,2:T(8,128)(2,1)S(1)}, u32[]{:S(2)}, u32[]{:S(2)}) %collective-permute-start.2) | collective-permute-done | bytes 65568 | tf_op jit(solution)/shard_map/ppermute | solution.py:15
  155.5 1.4 copy.44
  157.0 1.4 copy.45
  158.4 3.8 %multiply_convert_fusion = bf16[1024,8,80]{2,1,0:T(8,128)(2,1)S(1)} fusion(bf16[8,1024,4]{0,2,1:T(4,128)(2,1)} %copy.46, bf16[40,1024,4]{0,2,1:T(4,128)(2,1)} %copy.45, bf16[40,1024,4]{0,2,1:T(4,128)(2,1)} %copy.44), kind=kOutput, calls=%fused_computation.20 | convolution fusion | flops 7864320 | bytes 2031616 | tf_op jit(solution)/shard_map/dot_general | solution.py:70
  162.2 2.0 %copy.47 = bf16[1024,8,80]{0,2,1:T(8,128)(2,1)S(1)} copy(bf16[1024,8,80]{2,1,0:T(8,128)(2,1)S(1)} %multiply_convert_fusion) | data formatting | bytes 2621440 | tf_op jit(solution)/shard_map/convert_element_type | solution.py:115
  164.3 0.6 gather_fusion
  165.0 1.5 fusion.15
  (24 shorter events, 1.1 us)
Async XLA Ops:
  39.5 32.4 %copy-start = (bf16[2,17,2,8192]{3,2,1,0:T(2,128)(2,1)S(1)}, bf16[2,17,2,8192]{3,2,1,0:T(2,128)(2,1)}, u32[]{:S(2)}) copy-start(bf16[2,17,2,8192]{3,2,1,0:T(2,128)(2,1)} %param.2) | copy-start | bytes 3342340
  111.3 8.4 %all-to-all-start = ((bf16[4,2,4096]{2,1,0:T(2,128)(2,1)}), bf16[4,2,4096]{2,1,0:T(2,128)(2,1)S(1)}, u32[]{:S(2)}, u32[]{:S(2)}) async-start(bf16[4,2,4096]{2,1,0:T(2,128)(2,1)} %reshape.394), calls=%async_computation | async-start | bytes 131072 | tf_op jit(solution)/shard_map/all_to_all | solution.py:95
  139.6 7.3 %collective-permute-start = (bf16[1,8,1024,4]{2,1,3,0:T(8,128)(2,1)S(1)}, bf16[1,8,1024,4]{2,1,3,0:T(8,128)(2,1)S(1)}, u32[]{:S(2)}, u32[]{:S(2)}) collective-permute-start(bf16[1,8,1024,4]{2,1,3,0:T(8,128)(2,1)S(1)} %broadcast_in_dim_reshape.3), channel_id=1, source_target_pairs={{0,4},{4,8},{8,12},{12,16},{16,20},{20,24},{24,28},{28,0},{1,5},{5... | collective-permute-start | bytes 196616 | tf_op jit(solution)/shard_map/ppermute | solution.py:15
  146.9 8.6 %collective-permute-start.1 = (bf16[2,8,1024,4]{2,1,3,0:T(8,128)(2,1)S(1)}, bf16[2,8,1024,4]{2,1,3,0:T(8,128)(2,1)S(1)}, u32[]{:S(2)}, u32[]{:S(2)}) collective-permute-start(bf16[2,8,1024,4]{2,1,3,0:T(8,128)(2,1)S(1)} %pad_maximum_fusion.3), channel_id=1, source_target_pairs={{0,8},{4,12},{8,16},{12,20},{16,24},{20,28},{24,0},{28,4},{1,9},{5... | collective-permute-start | bytes 393224 | tf_op jit(solution)/shard_map/ppermute | solution.py:15
  147.5 8.0 %collective-permute-start.2 = (bf16[8,1024,4]{1,0,2:T(8,128)(2,1)S(1)}, bf16[8,1024,4]{1,0,2:T(8,128)(2,1)S(1)}, u32[]{:S(2)}, u32[]{:S(2)}) collective-permute-start(bf16[8,1024,4]{1,0,2:T(8,128)(2,1)S(1)} %reshape.350), channel_id=1, source_target_pairs={{0,16},{4,20},{8,24},{12,28},{16,0},{20,4},{24,8},{28,12},{1,17},{... | collective-permute-start | bytes 196616 | tf_op jit(solution)/shard_map/ppermute | solution.py:15
where the time goes:
time: 167 us; the launch traced here: 166 us
  other arithmetic  86.7 us (52%)
  local copies, waits for them, and re-layouts  41.5 us (25%)
  matrix products  17.5 us (10%)
  waiting for transfers between devices  11.6 us (7%)
  starting transfers between devices  8.94 us (5%)
    convert_element_type x1, other arithmetic, twiddles(): sines = jnp.sin(phase).astype(jnp.bfloat16)  35 us
    neg x1, other arithmetic, twiddles(): upper = jnp.concatenate([cosines, -sines], axis=1)  32.3 us
    unnamed x6, local copies, waits for them, and re-layouts  19.2 us
    dot_general x1, matrix products, channelise(): jnp.dot(lhs, table, preferred_element_type=jnp.float32)  13.7 us
    all_to_all x2, local copies, waits for them, and re-layouts, per_device(): lax.all_to_all(spectrum, 'chan', split_axis=1, concat_axis=0, tiled=True)  9.8 us
    ppermute x3, waiting for transfers between devices, from_behind(): lax.ppermute(value, axis, [(i, (i + by) % devices) for i in range(devices)])  9.25 us
    reshape x1, local copies, waits for them, and re-layouts, channelise(): return spectrum.reshape(count, ch_tot, 2, frames)  4.94 us
    another operation x1, other arithmetic, channelise(): lhs = jnp.stack([rot_real, rot_imag], axis=3).astype(jnp.bfloat16)  4.84 us
  transfers between devices with their start and end apart: 4, of which 3 were waited for; matrix products, arithmetic and copies ran while one was open for 2% of the time, Pallas kernels for 0%

commit v1 on v0

--- a/solution.py
+++ b/solution.py
@@ -92,7 +92,10 @@
     frames = samples.shape[1] - TAPS + 1
     cos_rot, sin_rot = rotations(ch_tot, DFT_BLOCK)
     spectrum = channelise(samples, taps_table(), twiddles(DFT_BLOCK), cos_rot, sin_rot, ch_tot)
-    local = lax.all_to_all(spectrum, "chan", split_axis=1, concat_axis=0, tiled=True)
+    local = jnp.concatenate(
+        lax.all_to_all(jnp.stack(jnp.split(spectrum, lax.axis_size("chan"), axis=1)), "chan", 0, 0),
+        axis=0,
+    )
     group_in = local.shape[0]
     own = local.reshape(group_in, CH_WIN, 2 * frames)
     keep_slots = n_stn // 2 + 1

time: 167 us -> 135 us (0.81)
  local copies, waits for them, and re-layouts: 41.5 us -> 9.1 us
    unnamed x6 -> x4, local copies, waits for them, and re-layouts: 19.2 us -> 1.37 us
    all_to_all x2 -> x0, local copies, waits for them, and re-layouts: 9.8 us -> none  [per_device(): lax.all_to_all(spectrum, 'chan', split_axis=1, concat_axis=0, tiled=True)]
    reshape x1, local copies, waits for them, and re-layouts: 4.94 us -> 0.02 us  [channelise(): return spectrum.reshape(count, ch_tot, 2, frames)]
    another operation x2 -> x3, other arithmetic: 4.58 us -> 5.32 us
  transfers between devices with their start and end apart: 4 -> 4, of which waited for: 3 -> 3; matrix products, arithmetic and copies ran while one was open for 2% -> 3% of each run, Pallas kernels for 0% -> 0%
where the time goes in v1:
time: 135 us
  other arithmetic  87.5 us (65%)
  matrix products  17.5 us (13%)
  waiting for transfers between devices  11.6 us (9%)
  starting transfers between devices  9.16 us (7%)
  local copies, waits for them, and re-layouts  9.1 us (7%)
    convert_element_type x1, other arithmetic, twiddles(): sines = jnp.sin(phase).astype(jnp.bfloat16)  35.1 us
    neg x1, other arithmetic, twiddles(): upper = jnp.concatenate([cosines, -sines], axis=1)  32.3 us
    dot_general x1, matrix products, channelise(): jnp.dot(lhs, table, preferred_element_type=jnp.float32)  13.7 us
    ppermute x3, waiting for transfers between devices, from_behind(): lax.ppermute(value, axis, [(i, (i + by) % devices) for i in range(devices)])  9.23 us
    ppermute x3, starting transfers between devices, from_behind(): lax.ppermute(value, axis, [(i, (i + by) % devices) for i in range(devices)])  4.9 us
    another operation x1, other arithmetic, channelise(): lhs = jnp.stack([rot_real, rot_imag], axis=3).astype(jnp.bfloat16)  4.84 us
    another operation x2, other arithmetic  4.58 us
    all_to_all x1, starting transfers between devices, per_device(): lax.all_to_all(jnp.stack(jnp.split(spectrum, lax.axis_size('chan'), axis=...  4.26 us
  transfers between devices with their start and end apart: 4, of which 3 were waited for; matrix products, arithmetic and copies ran while one was open for 3% of the time, Pallas kernels for 0%

profile of v1, /device:TPU:0, one launch (start us, length us, event | category | flops | bytes accessed | tf_op | source)
XLA Modules:
  0.0 135.0 jit_solution(623482681187098051)
XLA Ops:
  0.0 2.4 %fusion.29 = f32[131072]{0:T(1024)S(1)} fusion(), kind=kLoop, calls=%fused_computation.45 | loop fusion | flops 5373952 | bytes 524288 | tf_op jit(solution)/shard_map/mul | solution.py:22
  2.4 2.1 %fusion.41 = (f32[16,8192]{1,0:T(8,128)S(1)}, f32[16,8192]{1,0:T(8,128)S(1)}) fusion(), kind=kLoop, calls=%fused_computation.65 | loop fusion | flops 1966080 | bytes 1048576 | tf_op jit(solution)/shard_map/sin | solution.py:41
  4.5 35.1 %sine_convert_fusion = (bf16[8192,256]{1,0:T(8,128)(2,1)}, bf16[8192,256]{1,0:T(8,128)(2,1)}) fusion(), kind=kLoop, calls=%fused_computation.15 | loop fusion | flops 33554432 | bytes 8388608 | tf_op jit(solution)/shard_map/convert_element_type | solution.py:30
  39.5 32.3 %fusion.14 = bf16[8192,256]{1,0:T(8,128)(2,1)} fusion(), kind=kLoop, calls=%fused_computation.24 | loop fusion | flops 37748736 | bytes 4194304 | tf_op jit(solution)/shard_map/neg | solution.py:31
  71.9 2.1 %multiply_add_fusion.1 = f32[2,2,2,8192]{3,2,1,0:T(2,128)S(1)} fusion(bf16[2,17,2,8192]{3,2,1,0:T(2,128)(2,1)S(1)} %copy-done, f32[8192]{0:T(1024)S(1)} %get-tuple-element.19, f32[8192]{0:T(1024)S(1)} %get-tuple-element.20, f32[8192]{0:T(1024)S(1)} %get-tuple-element.21, f32[8192]{0:T(1024)S(1)} %get-tuple-element.22, f32[8192]{0:T(1024)S(1)} %get-tuple-element.23, ...), kind=kLoop, calls=%fused_computation.67 | loop fusion | flops 3080192 | bytes 2883584 | tf_op jit(solution)/shard_map/add | solution.py:51
  74.0 0.2 fusion.53
  74.2 0.2 copy_bitcast_fusion.1
  74.4 4.4 %add_convert_fusion = (bf16[16,2,2,1,8192]{4,3,2,1,0:T(2,128)(2,1)S(1)}, bf16[16,2,2,1,8192]{4,3,2,1,0:T(2,128)(2,1)S(1)}) fusion(f32[16,8192]{1,0:T(8,128)S(1)} %get-tuple-element.44, f32[2,2,8192]{2,1,0:T(2,128)S(1)} %get-tuple-element.42, f32[16,8192]{1,0:T(8,128)S(1)} %get-tuple-element.45, f32[2,2,8192]{2,1,0:T(2,128)S(1)} %get-tuple-element.43), kind=kLoop, calls=%fused_computation.23 | loop fusion | flops 4194304 | bytes 3407872 | tf_op jit(solution)/shard_map/convert
  78.8 4.8 %pad_maximum_fusion = bf16[16,2,2,2,8192]{4,3,2,1,0:T(2,128)(2,1)S(1)} fusion(bf16[16,2,2,1,8192]{4,3,2,1,0:T(2,128)(2,1)S(1)} %get-tuple-element.17, bf16[16,2,2,1,8192]{4,3,2,1,0:T(2,128)(2,1)S(1)} %get-tuple-element.16), kind=kLoop, calls=%fused_computation.21 | loop fusion | flops 4194304 | bytes 4194304 | tf_op jit(solution)/shard_map/stack | solution.py:58
  83.7 1.2 copy.55
  84.9 13.7 %fusion.19 = bf16[64,512]{1,0:T(8,128)(2,1)S(1)} fusion(bf16[64,16384]{1,0:T(8,128)(2,1)S(1)} %bitcast.55, bf16[8192,256]{1,0:T(8,128)(2,1)} %get-tuple-element.47, bf16[8192,256]{1,0:T(8,128)(2,1)} %get-tuple-element.46, bf16[8192,256]{1,0:T(8,128)(2,1)} %fusion.14), kind=kOutput, calls=%fused_computation.28 | convolution fusion | flops 1140916224 | bytes 14745600 | tf_op jit(solution)/shard_map/dot_general | solution.py:60
  98.7 0.7 pad_maximum_fusion.4
  99.5 4.3 %all-to-all-start = ((bf16[4,2,1024,2,2]{2,4,3,1,0:T(2,128)(2,1)}), bf16[4,2,1024,2,2]{2,4,3,1,0:T(2,128)(2,1)S(1)}, u32[]{:S(2)}, u32[]{:S(2)}) async-start(bf16[4,2,1024,2,2]{2,4,3,1,0:T(2,128)(2,1)} %pad_maximum_fusion.4), calls=%async_computation | async-start | bytes 131072 | tf_op jit(solution)/shard_map/all_to_all | solution.py:96
  103.7 0.7 fusion.51
  104.4 0.7 compare_bitcast_fusion
  105.1 0.2 reduce-window.7
  105.3 0.2 select_reduce_fusion
  105.5 2.3 %all-to-all-done = bf16[4,2,1024,2,2]{2,4,3,1,0:T(2,128)(2,1)S(1)} async-done(((bf16[4,2,1024,2,2]{2,4,3,1,0:T(2,128)(2,1)}), bf16[4,2,1024,2,2]{2,4,3,1,0:T(2,128)(2,1)S(1)}, u32[]{:S(2)}, u32[]{:S(2)}) %all-to-all-start) | async-done | bytes 65568 | tf_op jit(solution)/shard_map/all_to_all | solution.py:96
  107.9 2.2 %collective-permute-start = (bf16[1,8,1024,4]{2,1,3,0:T(8,128)(2,1)S(1)}, bf16[1,8,1024,4]{2,1,3,0:T(8,128)(2,1)S(1)}, u32[]{:S(2)}, u32[]{:S(2)}) collective-permute-start(bf16[1,8,1024,4]{2,1,3,0:T(8,128)(2,1)S(1)} %copy.51), channel_id=1, source_target_pairs={{0,4},{4,8},{8,12},{12,16},{16,20},{20,24},{24,28},{28,0},{1,5},{5... | collective-permute-start | bytes 196616 | tf_op jit(solution)/shard_map/ppermute | solution.py:15
  110.2 5.3 %collective-permute-done = bf16[1,8,1024,4]{2,1,3,0:T(8,128)(2,1)S(1)} collective-permute-done((bf16[1,8,1024,4]{2,1,3,0:T(8,128)(2,1)S(1)}, bf16[1,8,1024,4]{2,1,3,0:T(8,128)(2,1)S(1)}, u32[]{:S(2)}, u32[]{:S(2)}) %collective-permute-start) | collective-permute-done | bytes 65568 | tf_op jit(solution)/shard_map/ppermute | solution.py:15
  115.5 0.2 fusion.43
  115.8 0.1 broadcast_in_dim.76
  116.1 2.6 %collective-permute-start.2 = (bf16[8,1024,4]{1,0,2:T(8,128)(2,1)S(1)}, bf16[8,1024,4]{1,0,2:T(8,128)(2,1)S(1)}, u32[]{:S(2)}, u32[]{:S(2)}) collective-permute-start(bf16[8,1024,4]{1,0,2:T(8,128)(2,1)S(1)} %copy.49), channel_id=1, source_target_pairs={{0,16},{4,20},{8,24},{12,28},{16,0},{20,4},{24,8},{28,12},{1,17},{... | collective-permute-start | bytes 196616 | tf_op jit(solution)/shard_map/ppermute | solution.py:15
  118.7 1.4 %copy.45 = bf16[8,1024,4]{0,2,1:T(4,128)(2,1)} copy(bf16[8,1024,4]{1,2,0:T(4,128)(2,1)S(1)} %reshape.388) | data formatting | bytes 131072 | tf_op jit(solution)/shard_map/reshape;reshape | solution.py:100
  120.1 4.0 %collective-permute-done.2 = bf16[8,1024,4]{1,0,2:T(8,128)(2,1)S(1)} collective-permute-done((bf16[8,1024,4]{1,0,2:T(8,128)(2,1)S(1)}, bf16[8,1024,4]{1,0,2:T(8,128)(2,1)S(1)}, u32[]{:S(2)}, u32[]{:S(2)}) %collective-permute-start.2) | collective-permute-done | bytes 65568 | tf_op jit(solution)/shard_map/ppermute | solution.py:15
  124.1 1.4 %copy.43 = bf16[40,1024,4]{0,2,1:T(4,128)(2,1)} copy(bf16[40,1024,4]{1,0,2:T(8,128)(2,1)S(1)} %copy_bitcast_fusion) | data formatting | bytes 655360 | tf_op jit(solution)/shard_map/reshape | solution.py:117
  125.5 1.4 %copy.44 = bf16[40,1024,4]{0,2,1:T(4,128)(2,1)} copy(bf16[40,1024,4]{1,0,2:T(8,128)(2,1)S(1)} %pad_maximum_fusion.2) | data formatting | bytes 655360 | tf_op jit(solution)/shard_map/concatenate | solution.py:68
  127.0 3.8 %multiply_convert_fusion = bf16[1024,8,80]{2,1,0:T(8,128)(2,1)S(1)} fusion(bf16[8,1024,4]{0,2,1:T(4,128)(2,1)} %copy.45, bf16[40,1024,4]{0,2,1:T(4,128)(2,1)} %copy.44, bf16[40,1024,4]{0,2,1:T(4,128)(2,1)} %copy.43), kind=kOutput, calls=%fused_computation.20 | convolution fusion | flops 7864320 | bytes 2031616 | tf_op jit(solution)/shard_map/dot_general | solution.py:70
  130.7 2.0 %copy.46 = bf16[1024,8,80]{0,2,1:T(8,128)(2,1)S(1)} copy(bf16[1024,8,80]{2,1,0:T(8,128)(2,1)S(1)} %multiply_convert_fusion) | data formatting | bytes 2621440 | tf_op jit(solution)/shard_map/convert_element_type | solution.py:118
  132.7 0.1 copy.47
  132.9 0.6 gather_fusion
  133.5 1.5 %fusion.15 = bf16[8,2,1024,40]{2,3,1,0:T(8,128)(2,1)} fusion(pred[40]{0:T(512)(128)(4,1)S(1)} %broadcast_in_dim.76, pred[40]{0:T(512)(128)(4,1)S(1)} %broadcast_in_dim.71, bf16[5,8,2,1024,8]{3,4,2,1,0:T(8,128)(2,1)S(1)} %gather_fusion), kind=kLoop, calls=%fused_computation.26 | loop fusion | flops 1310720 | bytes 2621520 | tf_op jit(solution)/shard_map/jit(_where)/select_n | solution.py:122
  (24 shorter events, 0.7 us)
Async XLA Ops:
  39.5 32.4 %copy-start = (bf16[2,17,2,8192]{3,2,1,0:T(2,128)(2,1)S(1)}, bf16[2,17,2,8192]{3,2,1,0:T(2,128)(2,1)}, u32[]{:S(2)}) copy-start(bf16[2,17,2,8192]{3,2,1,0:T(2,128)(2,1)} %param.2) | copy-start | bytes 3342340
  99.5 8.4 %all-to-all-start = ((bf16[4,2,1024,2,2]{2,4,3,1,0:T(2,128)(2,1)}), bf16[4,2,1024,2,2]{2,4,3,1,0:T(2,128)(2,1)S(1)}, u32[]{:S(2)}, u32[]{:S(2)}) async-start(bf16[4,2,1024,2,2]{2,4,3,1,0:T(2,128)(2,1)} %pad_maximum_fusion.4), calls=%async_computation | async-start | bytes 131072 | tf_op jit(solution)/shard_map/all_to_all | solution.py:96
  107.9 7.5 %collective-permute-start = (bf16[1,8,1024,4]{2,1,3,0:T(8,128)(2,1)S(1)}, bf16[1,8,1024,4]{2,1,3,0:T(8,128)(2,1)S(1)}, u32[]{:S(2)}, u32[]{:S(2)}) collective-permute-start(bf16[1,8,1024,4]{2,1,3,0:T(8,128)(2,1)S(1)} %copy.51), channel_id=1, source_target_pairs={{0,4},{4,8},{8,12},{12,16},{16,20},{20,24},{24,28},{28,0},{1,5},{5... | collective-permute-start | bytes 196616 | tf_op jit(solution)/shard_map/ppermute | solution.py:15
  115.4 8.6 %collective-permute-start.1 = (bf16[2,8,1024,4]{2,1,3,0:T(8,128)(2,1)S(1)}, bf16[2,8,1024,4]{2,1,3,0:T(8,128)(2,1)S(1)}, u32[]{:S(2)}, u32[]{:S(2)}) collective-permute-start(bf16[2,8,1024,4]{2,1,3,0:T(8,128)(2,1)S(1)} %pad_maximum_fusion.3), channel_id=1, source_target_pairs={{0,8},{4,12},{8,16},{12,20},{16,24},{20,28},{24,0},{28,4},{1,9},{5... | collective-permute-start | bytes 393224 | tf_op jit(solution)/shard_map/ppermute | solution.py:15
  116.1 8.0 %collective-permute-start.2 = (bf16[8,1024,4]{1,0,2:T(8,128)(2,1)S(1)}, bf16[8,1024,4]{1,0,2:T(8,128)(2,1)S(1)}, u32[]{:S(2)}, u32[]{:S(2)}) collective-permute-start(bf16[8,1024,4]{1,0,2:T(8,128)(2,1)S(1)} %copy.49), channel_id=1, source_target_pairs={{0,16},{4,20},{8,24},{12,28},{16,0},{20,4},{24,8},{28,12},{1,17},{... | collective-permute-start | bytes 196616 | tf_op jit(solution)/shard_map/ppermute | solution.py:15
